TPU v7x, 32 devices: a whole 2x2x4 slice. The times are simulated.
32 devices in a mesh: groups: 2 (over y), blk: 4 (over z), dp: 2 (over x), sub: 2 (over core).
Axes of the slice: x: 2, y: 2, z: 4, core: 2. Of those that a mesh axis runs over, the one named last changes fastest.
Arguments:
- view_a: bfloat16 [2048, 256], P(('groups', 'blk', 'dp', 'sub')), parts along dimension 0, may hold values from -6 to 6
- view_b: bfloat16 [2048, 256], P(('groups', 'blk', 'dp', 'sub')), parts along dimension 0, may hold values from -6 to 6
- prototypes: bfloat16 [32768, 256], P('blk'), may hold values from -6 to 6
- tile_mask: int32 [16, 256], replicated, may hold values from 0 to 1, as said below
- tile_region: int32 [32], P('groups'), parts along dimension 0, may hold values from 0 to 15, as said below
Outputs:
- grad_view_b: float32 [2048, 256], P(('groups', 'blk', 'dp', 'sub')), parts along dimension 0
- grad_prototypes: float32 [65536, 256], P(('groups', 'blk', 'dp', 'sub')), parts along dimension 0
There are 2 independent parts, one for each index of `groups`. A program takes and returns all parts, laid end to end along the dimension named above; an argument that names none is the same for every part. Nothing has to cross between parts.
Inputs may be any that keep to these rules, and one draw needn't show every extreme that they name: `tile_mask`: every prototype tile is 1 for at least one region, and every region for at least 16 tiles. `tile_region`: every region is named by at least one hit tile.
All inputs are finite; a program needn't handle non-finite values.
Results may differ from a plain program's by a relative error of at most 0.00045.
The roundings to bfloat16 on the way count: a program that leaves them out, or rounds other values in their place, can miss the bound.
Values may be sent and summed in bfloat16 or wider, within the bound.
A program may use at most 64 MiB of HBM per device.

v0:
```python
import jax
import jax.numpy as jnp
from jax import lax
from jax.sharding import PartitionSpec as P

TILE = 128
ITERS = 3
SOFTMAX_TEMPER = 0.1
EPSILON = 0.05


def from_behind(block, axis, distance):
    devices = range(lax.axis_size(axis))
    route = [((i - distance) % len(devices), i) for i in devices]
    return lax.ppermute(block, axis, route)


def unit_rows(matrix):
    values = matrix.astype(jnp.float32)
    return (values * lax.rsqrt(jnp.sum(values * values, axis=1, keepdims=True) + 1e-06)).astype(
        jnp.bfloat16
    )


def to_global(vector, blk_pos, block_count):
    return jnp.roll(vector[::-1], blk_pos + 1 - block_count, axis=0)


def body(view_a, view_b, prototypes, tile_mask, tile_region):
    n_blk = lax.axis_size("blk")
    n_dp = lax.axis_size("dp")
    n_sub = lax.axis_size("sub")
    blk_pos = lax.axis_index("blk")
    dp_pos = lax.axis_index("dp")
    sub_pos = lax.axis_index("sub")
    hit_dev = view_a.shape[0]
    block_rows = prototypes.shape[0]
    share_cols = block_rows // n_dp
    tiles_share = share_cols // TILE
    tiles_block = block_rows // TILE
    regions = tile_mask.shape[0]
    own_block = unit_rows(lax.dynamic_slice_in_dim(prototypes, dp_pos * share_cols, share_cols, 0))
    unit_a = unit_rows(view_a)
    unit_b = unit_rows(view_b)
    rows_a, rows_b = (
        lax.all_gather(unit_a, "dp", axis=0, tiled=True),
        lax.all_gather(unit_b, "dp", axis=0, tiled=True),
    )
    detector_hit_rows = rows_a.shape[0]
    both_rows = jnp.concatenate([rows_a, rows_b], axis=0)
    region_grid = tile_region.reshape(n_blk, n_dp, n_sub)
    my_regions = lax.dynamic_index_in_dim(
        lax.dynamic_index_in_dim(region_grid, blk_pos, 0, keepdims=False),
        sub_pos,
        1,
        keepdims=False,
    )
    onehot = (my_regions[:, None] == jnp.arange(regions, dtype=jnp.int32)[None, :]).astype(
        jnp.float32
    )
    row_tiles = jnp.dot(onehot, tile_mask.astype(jnp.float32))

    def active_at(block_id):
        tile_flags = lax.dynamic_slice_in_dim(
            row_tiles, block_id * tiles_block + dp_pos * tiles_share, tiles_share, 1
        )
        expanded = jnp.broadcast_to(
            tile_flags[:, None, :, None] > 0.5, (n_dp, hit_dev, tiles_share, TILE)
        )
        return expanded.reshape(detector_hit_rows, share_cols)

    def forward(proto_block, block_id):
        prototype_scores = jnp.einsum(
            "rd,kd->rk", both_rows, proto_block, preferred_element_type=jnp.float32
        )
        live_block_mask = active_at(block_id)
        code_exp = jnp.where(
            live_block_mask, jnp.exp((prototype_scores[:detector_hit_rows] - 1.0) / EPSILON), 0.0
        ).astype(jnp.bfloat16)
        prototype_weights = jnp.where(
            live_block_mask,
            jnp.exp((prototype_scores[detector_hit_rows:] - 1.0) / SOFTMAX_TEMPER),
            0.0,
        )
        return (
            code_exp,
            jnp.sum(code_exp.astype(jnp.float32), axis=0),
            jnp.sum(prototype_weights, axis=1),
        )

    code_first, colsum_first, norm_first = forward(own_block, blk_pos)
    code_stack = (
        jnp.zeros((n_blk, detector_hit_rows, share_cols), jnp.bfloat16).at[0].set(code_first)
    )
    colsum_stack = jnp.zeros((n_blk, share_cols), jnp.float32).at[0].set(colsum_first)
    block_stack = jnp.zeros((1,), jnp.bfloat16)

    def forward_turn(carry_state, turn_index):
        proto_block, code_all, colsum_all, blocks_all, norm_part = carry_state
        proto_block = from_behind(proto_block, "blk", 1)
        block_id = (blk_pos - turn_index) % n_blk
        code_exp, colsum, norm_add = forward(proto_block, block_id)
        code_all = lax.dynamic_update_index_in_dim(code_all, code_exp, turn_index, 0)
        colsum_all = lax.dynamic_update_index_in_dim(colsum_all, colsum, turn_index, 0)
        return ((proto_block, code_all, colsum_all, blocks_all, norm_part + norm_add), None)

    turns = jnp.arange(1, n_blk, dtype=jnp.int32)
    carry_state, unused = lax.scan(
        forward_turn, (own_block, code_stack, colsum_stack, block_stack, norm_first), turns
    )
    code_all = carry_state[1]
    colsum_all = carry_state[2]
    blocks_all = carry_state[3]
    norm_part = carry_state[4]

    def column_recip(colsum_steps):
        global_sums = to_global(colsum_steps, blk_pos, n_blk).reshape(-1)
        totals = lax.psum(global_sums, ("blk", "sub"))
        recip_vec = 1.0 / totals
        return to_global(recip_vec.reshape(n_blk, share_cols), blk_pos, n_blk)

    def row_partial(column_inverses):
        return jnp.sum(code_all.astype(jnp.float32) * column_inverses[:, None, :], axis=(0, 2))

    column_inverses = column_recip(colsum_all)
    row_totals, second_view_norm = lax.psum((row_partial(column_inverses), norm_part), "dp")
    row_inverses = 1.0 / row_totals
    for sweep_index in range(ITERS - 1):
        colsum_all = jnp.sum(code_all.astype(jnp.float32) * row_inverses[None, :, None], axis=1)
        column_inverses = column_recip(colsum_all)
        row_inverses = 1.0 / lax.psum(row_partial(column_inverses), "dp")

    def backward(proto_block, turn_index, block_id):
        prototype_scores = jnp.einsum(
            "rd,kd->rk", rows_b, proto_block, preferred_element_type=jnp.float32
        )
        live_block_mask = active_at(block_id)
        predicted_logits = (
            jnp.where(live_block_mask, jnp.exp((prototype_scores - 1.0) / SOFTMAX_TEMPER), 0.0)
            / second_view_norm[:, None]
        )
        code_exp = lax.dynamic_index_in_dim(code_all, turn_index, 0, keepdims=False).astype(
            jnp.float32
        )
        col_vals = lax.dynamic_index_in_dim(column_inverses, turn_index, 0, keepdims=False)
        code_entries = row_inverses[:, None] * code_exp * col_vals[None, :]
        score_gradient = ((predicted_logits - code_entries) / SOFTMAX_TEMPER).astype(jnp.bfloat16)
        hit_part = jnp.dot(score_gradient, proto_block, preferred_element_type=jnp.float32)
        proto_part = jnp.einsum(
            "rk,rd->kd", score_gradient, rows_b, preferred_element_type=jnp.float32
        )
        return (hit_part, proto_part)

    def pass_grads(running):
        return from_behind(running, "blk", 1)

    hit_first, proto_first = backward(own_block, 0, blk_pos)

    def backward_turn(carry_state, turn_index):
        proto_block, hit_running, proto_running = carry_state
        block_id = (blk_pos - turn_index) % n_blk
        proto_block = from_behind(proto_block, "blk", 1)
        proto_running = pass_grads(proto_running)
        hit_part, proto_part = backward(proto_block, turn_index, block_id)
        return ((proto_block, hit_running + hit_part, proto_running + proto_part), None)

    carry_state, unused = lax.scan(backward_turn, (own_block, hit_first, proto_first), turns)
    proto_home = pass_grads(carry_state[2])
    grad_view_b = lax.psum_scatter(carry_state[1], "dp", scatter_dimension=0, tiled=True)
    grad_prototypes = lax.psum_scatter(proto_home, "sub", scatter_dimension=0, tiled=True)
    return (grad_view_b, grad_prototypes)


def solution(mesh):
    placed = (
        P(("groups", "blk", "dp", "sub"), None),
        P(("groups", "blk", "dp", "sub"), None),
        P("blk", None),
        P(),
        P("groups"),
    )
    return jax.shard_map(
        body,
        mesh=mesh,
        in_specs=placed,
        out_specs=(
            P(("groups", "blk", "dp", "sub"), None),
            P(("groups", "blk", "dp", "sub"), None),
        ),
        check_vma=False,
    )
```

profile of v0, /device:TPU:0, one launch (start us, length us, event | category | flops | bytes accessed | tf_op | source)
XLA Modules:
  0.0 934.0 jit_solution(10555834925362059622)
XLA Ops:
  8.0 2.2 fusion.28
  10.2 1.9 fusion.29
  12.4 5.5 all_gather.6
  18.1 4.6 all_gather.7
  22.7 1.4 copy.37
  24.1 2.7 fusion.61
  27.5 3.4 fusion.33
  30.9 2.4 scatter.6
  33.3 155.7 %while.37 = (s32[]{:T(128)}, bf16[4096,256]{1,0:T(8,128)(2,1)}, bf16[4,128,4096]{2,1,0:T(8,128)(2,1)}, f32[4,4096]{1,0:T(4,128)S(1)}, f32[128]{0:T(128)S(1)}, /*...) while((s32[]{:T(128)}, bf16[4096,256]{1,0:T(8,128)(2,1)}, ...), condition=%wide.region_8.9_spmd, body=%wide.region_5.8_spmd.sunk | while | flops 544206912 | bytes 27970340 | solution.py:108
  33.3 2.2 collective-permute-start
  38.9 42.1 %collective-permute-done = bf16[4096,256]{1,0:T(8,128)(2,1)S(1)} collective-permute-done((bf16[4096,256]{1,0:T(8,128)(2,1)}, bf16[4096,256]{1,0:T(8,128)(2,1)S(1)}, u32[]{:S(2)}, u32[]{:S(2)}) %collective-permute-start) | collective-permute-done | bytes 2097184 | tf_op jit(solution)/shard_map/while/body/eval_jaxpr/ppermute | solution.py:15
  83.2 1.6 bitcast_dynamic-update-slice_fusion.2
  85.0 1.4 copy.47
  89.8 43.0 %collective-permute-done = bf16[4096,256]{1,0:T(8,128)(2,1)S(1)} collective-permute-done((bf16[4096,256]{1,0:T(8,128)(2,1)}, bf16[4096,256]{1,0:T(8,128)(2,1)S(1)}, u32[]{:S(2)}, u32[]{:S(2)}) %collective-permute-start) | collective-permute-done | bytes 2097184 | tf_op jit(solution)/shard_map/while/body/eval_jaxpr/ppermute | solution.py:15
  134.9 1.6 bitcast_dynamic-update-slice_fusion.2
  136.8 1.4 copy.47
  141.6 42.1 %collective-permute-done = bf16[4096,256]{1,0:T(8,128)(2,1)S(1)} collective-permute-done((bf16[4096,256]{1,0:T(8,128)(2,1)}, bf16[4096,256]{1,0:T(8,128)(2,1)S(1)}, u32[]{:S(2)}, u32[]{:S(2)}) %collective-permute-start) | collective-permute-done | bytes 2097184 | tf_op jit(solution)/shard_map/while/body/eval_jaxpr/ppermute | solution.py:15
  185.8 1.6 bitcast_dynamic-update-slice_fusion.2
  187.6 1.4 copy.47
  190.5 51.5 %all-reduce.7.cloned.1.call-done = f32[16384]{0:T(1024)} async-done(((f32[16384]{0:T(1024)}), f32[16384]{0:T(1024)}) %all-reduce.7.cloned.1.call-update) | async-done | bytes 65552 | tf_op jit(solution)/shard_map/psum | solution.py:118
  243.8 3.1 fusion.16
  246.9 4.9 psum.51
  251.8 3.2 fusion.17
  256.6 52.7 %all-reduce.9.cloned.1.call-done = f32[16384]{0:T(1024)} async-done(((f32[16384]{0:T(1024)}), f32[16384]{0:T(1024)}) %all-reduce.9.cloned.1.call-update) | async-done | bytes 65552 | tf_op jit(solution)/shard_map/psum | solution.py:118
  311.1 3.1 fusion.18
  314.2 4.9 psum.53
  319.1 3.2 fusion.19
  324.1 52.5 %all-reduce.11.cloned.1.call-done = f32[16384]{0:T(1024)} async-done(((f32[16384]{0:T(1024)}), f32[16384]{0:T(1024)}) %all-reduce.11.cloned.1.call-update) | async-done | bytes 65552 | tf_op jit(solution)/shard_map/psum | solution.py:118
  378.4 3.2 fusion.20
  381.6 4.9 all-reduce.2
  386.6 2.5 fusion.27
  389.1 2.7 fusion.63
  392.3 435.9 %while.38 = (s32[]{:T(128)}, bf16[4096,256]{1,0:T(8,128)(2,1)S(1)}, f32[128,256]{1,0:T(8,128)S(1)}, f32[4096,256]{1,0:T(8,128)}, s32[3]{0:T(128)S(1)}, /*index=5...) while((s32[]{:T(128)}, bf16[4096,256]{1,0:T(8,128)(2,1)S(1)}, ...), condition=%wide.region_22.24_spmd, body=%wide.region_21.23_spmd.sunk | while | flops 811630720 | bytes 64407448 | solution.py:167
  397.7 131.2 %collective-permute-done.1 = bf16[4096,256]{1,0:T(8,128)(2,1)S(1)} collective-permute-done((bf16[4096,256]{1,0:T(8,128)(2,1)}, bf16[4096,256]{1,0:T(8,128)(2,1)S(1)}, u32[]{:S(2)}, u32[]{:S(2)}) %collective-permute-start.1) | collective-permute-done | bytes 2097184 | tf_op jit(solution)/shard_map/while/body/eval_jaxpr/ppermute | solution.py:15
  528.9 1.3 copy.63
  530.5 2.5 fusion.101
  533.5 5.1 convolution_add_fusion.7
  538.6 1.3 copy-done.2
  543.2 131.0 %collective-permute-done.1 = bf16[4096,256]{1,0:T(8,128)(2,1)S(1)} collective-permute-done((bf16[4096,256]{1,0:T(8,128)(2,1)}, bf16[4096,256]{1,0:T(8,128)(2,1)S(1)}, u32[]{:S(2)}, u32[]{:S(2)}) %collective-permute-start.1) | collective-permute-done | bytes 2097184 | tf_op jit(solution)/shard_map/while/body/eval_jaxpr/ppermute | solution.py:15
  674.2 1.3 copy.63
  675.7 2.5 fusion.101
  678.8 5.1 convolution_add_fusion.7
  688.5 130.1 %collective-permute-done.1 = bf16[4096,256]{1,0:T(8,128)(2,1)S(1)} collective-permute-done((bf16[4096,256]{1,0:T(8,128)(2,1)}, bf16[4096,256]{1,0:T(8,128)(2,1)S(1)}, u32[]{:S(2)}, u32[]{:S(2)}) %collective-permute-start.1) | collective-permute-done | bytes 2097184 | tf_op jit(solution)/shard_map/while/body/eval_jaxpr/ppermute | solution.py:15
  818.5 1.3 copy.63
  820.1 2.5 fusion.101
  823.1 5.1 convolution_add_fusion.7
  828.9 88.2 %collective-permute-done.3 = f32[4096,256]{1,0:T(8,128)} collective-permute-done((f32[4096,256]{1,0:T(8,128)}, f32[4096,256]{1,0:T(8,128)}, u32[]{:S(2)}, u32[]{:S(2)}) %collective-permute-start.3) | collective-permute-done | bytes 4194336 | tf_op jit(solution)/shard_map/ppermute | solution.py:15
  917.2 10.3 %reduce-scatter.5.cloned.1.call-done = f32[2048,256]{1,0:T(8,128)} async-done(((f32[4096,256]{1,0:T(8,128)}), f32[2048,256]{1,0:T(8,128)}) %reduce-scatter.5.cloned.1.call-update) | async-done | bytes 2097168 | tf_op jit(solution)/shard_map/reduce_scatter | solution.py:170
  (124 shorter events, 29.6 us)
Async XLA Ops:
  7.2 234.9 %all-reduce.7.cloned.1.call-start = ((), (), s32[]{:S(2)}) async-start(), calls=%async_computation.2 | async-start | bytes 131072 | tf_op jit(solution)/shard_map/psum | solution.py:118
  10.2 2.0 copy-start.5
  10.2 7.7 copy-start.6
  12.2 11.9 %copy-start = (bf16[4096,256]{1,0:T(8,128)(2,1)}, bf16[4096,256]{1,0:T(8,128)(2,1)S(1)}, u32[]{:S(2)}) copy-start(bf16[4096,256]{1,0:T(8,128)(2,1)S(1)} %fusion.29) | copy-start | bytes 6291460
  24.1 2.9 copy-start.7
  33.3 47.7 %collective-permute-start = (bf16[4096,256]{1,0:T(8,128)(2,1)}, bf16[4096,256]{1,0:T(8,128)(2,1)S(1)}, u32[]{:S(2)}, u32[]{:S(2)}) collective-permute-start(bf16[4096,256]{1,0:T(8,128)(2,1)} %get-tuple-element.575), channel_id=1, source_target_pairs={{12,0},{0,4},{4,8},{8,12},{13,1},{1,5},{5,9},{9,13},{14,2},{2,6},{... | collective-permute-start | bytes 6291464 | tf_op jit(solution)/shard_map/while/body/eval_jaxpr/ppermute | solution.py:15
  86.4 46.4 %collective-permute-start = (bf16[4096,256]{1,0:T(8,128)(2,1)}, bf16[4096,256]{1,0:T(8,128)(2,1)S(1)}, u32[]{:S(2)}, u32[]{:S(2)}) collective-permute-start(bf16[4096,256]{1,0:T(8,128)(2,1)} %get-tuple-element.575), channel_id=1, source_target_pairs={{12,0},{0,4},{4,8},{8,12},{13,1},{1,5},{5,9},{9,13},{14,2},{2,6},{... | collective-permute-start | bytes 6291464 | tf_op jit(solution)/shard_map/while/body/eval_jaxpr/ppermute | solution.py:15
  138.2 45.5 %collective-permute-start = (bf16[4096,256]{1,0:T(8,128)(2,1)}, bf16[4096,256]{1,0:T(8,128)(2,1)S(1)}, u32[]{:S(2)}, u32[]{:S(2)}) collective-permute-start(bf16[4096,256]{1,0:T(8,128)(2,1)} %get-tuple-element.575), channel_id=1, source_target_pairs={{12,0},{0,4},{4,8},{8,12},{13,1},{1,5},{5,9},{9,13},{14,2},{2,6},{... | collective-permute-start | bytes 6291464 | tf_op jit(solution)/shard_map/while/body/eval_jaxpr/ppermute | solution.py:15
  190.5 118.8 %all-reduce.9.cloned.1.call-start = ((), (), s32[]{:S(2)}) async-start(), calls=%async_computation.3 | async-start | bytes 131072 | tf_op jit(solution)/shard_map/psum | solution.py:118
  256.6 120.0 %all-reduce.11.cloned.1.call-start = ((), (), s32[]{:S(2)}) async-start(), calls=%async_computation.4 | async-start | bytes 131072 | tf_op jit(solution)/shard_map/psum | solution.py:118
  323.9 593.3 %reduce-scatter.3.cloned.1.call-start = ((), (), s32[]{:S(2)}) async-start(), calls=%async_computation.5 | async-start | bytes 196608 | tf_op jit(solution)/shard_map/reduce_scatter | solution.py:169
  378.4 8.2 copy-start.1
  392.3 1.3 copy-start.2
  392.4 141.1 %collective-permute-start.2 = (f32[4096,256]{1,0:T(8,128)}, f32[4096,256]{1,0:T(8,128)}, u32[]{:S(2)}, u32[]{:S(2)}) collective-permute-start(f32[4096,256]{1,0:T(8,128)} %get-tuple-element.628), channel_id=1, source_target_pairs={{12,0},{0,4},{4,8},{8,12},{13,1},{1,5},{5,9},{9,13},{14,2},{2,6},{... | collective-permute-start | bytes 12582920 | tf_op jit(solution)/shard_map/while/body/eval_jaxpr/ppermute | solution.py:15
  393.7 135.3 %collective-permute-start.1 = (bf16[4096,256]{1,0:T(8,128)(2,1)}, bf16[4096,256]{1,0:T(8,128)(2,1)S(1)}, u32[]{:S(2)}, u32[]{:S(2)}) collective-permute-start(bf16[4096,256]{1,0:T(8,128)(2,1)} %copy-done.2), channel_id=1, source_target_pairs={{12,0},{0,4},{4,8},{8,12},{13,1},{1,5},{5,9},{9,13},{14,2},{2,6},{... | collective-permute-start | bytes 6291464 | tf_op jit(solution)/shard_map/while/body/eval_jaxpr/ppermute | solution.py:15
  533.5 5.1 copy-start.3
  538.6 1.3 copy-start.2
  538.6 140.2 %collective-permute-start.2 = (f32[4096,256]{1,0:T(8,128)}, f32[4096,256]{1,0:T(8,128)}, u32[]{:S(2)}, u32[]{:S(2)}) collective-permute-start(f32[4096,256]{1,0:T(8,128)} %get-tuple-element.628), channel_id=1, source_target_pairs={{12,0},{0,4},{4,8},{8,12},{13,1},{1,5},{5,9},{9,13},{14,2},{2,6},{... | collective-permute-start | bytes 12582920 | tf_op jit(solution)/shard_map/while/body/eval_jaxpr/ppermute | solution.py:15
  539.9 134.3 %collective-permute-start.1 = (bf16[4096,256]{1,0:T(8,128)(2,1)}, bf16[4096,256]{1,0:T(8,128)(2,1)S(1)}, u32[]{:S(2)}, u32[]{:S(2)}) collective-permute-start(bf16[4096,256]{1,0:T(8,128)(2,1)} %copy-done.2), channel_id=1, source_target_pairs={{12,0},{0,4},{4,8},{8,12},{13,1},{1,5},{5,9},{9,13},{14,2},{2,6},{... | collective-permute-start | bytes 6291464 | tf_op jit(solution)/shard_map/while/body/eval_jaxpr/ppermute | solution.py:15
  678.8 5.1 copy-start.3
  683.9 1.3 copy-start.2
  683.9 139.2 %collective-permute-start.2 = (f32[4096,256]{1,0:T(8,128)}, f32[4096,256]{1,0:T(8,128)}, u32[]{:S(2)}, u32[]{:S(2)}) collective-permute-start(f32[4096,256]{1,0:T(8,128)} %get-tuple-element.628), channel_id=1, source_target_pairs={{12,0},{0,4},{4,8},{8,12},{13,1},{1,5},{5,9},{9,13},{14,2},{2,6},{... | collective-permute-start | bytes 12582920 | tf_op jit(solution)/shard_map/while/body/eval_jaxpr/ppermute | solution.py:15
  685.2 133.4 %collective-permute-start.1 = (bf16[4096,256]{1,0:T(8,128)(2,1)}, bf16[4096,256]{1,0:T(8,128)(2,1)S(1)}, u32[]{:S(2)}, u32[]{:S(2)}) collective-permute-start(bf16[4096,256]{1,0:T(8,128)(2,1)} %copy-done.2), channel_id=1, source_target_pairs={{12,0},{0,4},{4,8},{8,12},{13,1},{1,5},{5,9},{9,13},{14,2},{2,6},{... | collective-permute-start | bytes 6291464 | tf_op jit(solution)/shard_map/while/body/eval_jaxpr/ppermute | solution.py:15
  823.1 5.1 copy-start.3
  828.2 0.6 copy-start.4
  828.2 88.9 %collective-permute-start.3 = (f32[4096,256]{1,0:T(8,128)}, f32[4096,256]{1,0:T(8,128)}, u32[]{:S(2)}, u32[]{:S(2)}) collective-permute-start(f32[4096,256]{1,0:T(8,128)} %get-tuple-element.360), channel_id=1, source_target_pairs={{12,0},{0,4},{4,8},{8,12},{13,1},{1,5},{5,9},{9,13},{14,2},{2,6},{... | collective-permute-start | bytes 12582920 | tf_op jit(solution)/shard_map/ppermute | solution.py:15
  828.9 98.6 %reduce-scatter.5.cloned.1.call-start = ((), (), s32[]{:S(2)}) async-start(), calls=%async_computation.6 | async-start | bytes 6291456 | tf_op jit(solution)/shard_map/reduce_scatter | solution.py:170
Sparse Core Ops, SparseCore 0:
  190.6 51.3 all-reduce.6
  256.7 52.5 all-reduce.8
  324.0 52.5 all-reduce.10
  829.0 11.0 reduce-scatter.2
  917.3 10.2 reduce-scatter.4
where the time goes:
time: 935 us; the launch traced here: 934 us
  waiting for transfers between devices  775 us (83%)
  other arithmetic  35.5 us (4%)
  matrix products  35.1 us (4%)
  local copies, waits for them, and re-layouts  29.5 us (3%)
  blocking collectives  24.9 us (3%)
  loops' own time  16.2 us (2%)
  between operations  14.1 us (2%)
    ppermute x10, waiting for transfers between devices, from_behind(): return lax.ppermute(block, axis, route)  608 us
    psum x3, waiting for transfers between devices, column_recip(): totals = lax.psum(global_sums, ('blk', 'sub'))  157 us
  transfers between devices with their start and end apart: 15, of which 11 were waited for; matrix products, arithmetic and copies ran while one was open for 2% of the time, Pallas kernels for 0%

commit v1 on v0

--- a/solution.py
+++ b/solution.py
@@ -115,7 +115,7 @@
 
     def column_recip(colsum_steps):
         global_sums = to_global(colsum_steps, blk_pos, n_blk).reshape(-1)
-        totals = lax.psum(global_sums, ("blk", "sub"))
+        totals = lax.all_gather(global_sums, ("blk", "sub")).sum(axis=0)
         recip_vec = 1.0 / totals
         return to_global(recip_vec.reshape(n_blk, share_cols), blk_pos, n_blk)
 

time: 935 us -> 828 us (0.89)
  waiting for transfers between devices: 775 us -> 627 us
  blocking collectives: 24.9 us -> 70.1 us
    psum x3 -> x0, waiting for transfers between devices: 157 us -> none  [column_recip(): totals = lax.psum(global_sums, ('blk', 'sub'))]
    all_gather x0 -> x3, blocking collectives: none -> 45.2 us  [column_recip(): totals = lax.all_gather(global_sums, ('blk', 'sub')).sum(axis=0)]
  transfers between devices with their start and end apart: 15 -> 12, of which waited for: 11 -> 8; matrix products, arithmetic and copies ran while one was open for 2% -> 2% of each run, Pallas kernels for 0% -> 0%
where the time goes in v1:
time: 828 us
  waiting for transfers between devices  627 us (76%)
  blocking collectives  70.1 us (8%)
  matrix products  35.1 us (4%)
  other arithmetic  34.1 us (4%)
  local copies, waits for them, and re-layouts  28.6 us (3%)
  loops' own time  15.9 us (2%)
  between operations  14.4 us (2%)
    ppermute x10, waiting for transfers between devices, from_behind(): return lax.ppermute(block, axis, route)  617 us
    all_gather x3, blocking collectives, column_recip(): totals = lax.all_gather(global_sums, ('blk', 'sub')).sum(axis=0)  45.2 us
    dot_general x4, matrix products, backward(): jnp.einsum('rk,rd->kd', score_gradient, rows_b, preferred_element_type=jn...  18 us
  transfers between devices with their start and end apart: 12, of which 8 were waited for; matrix products, arithmetic and copies ran while one was open for 2% of the time, Pallas kernels for 0%

profile of v1, /device:TPU:0, one launch (start us, length us, event | category | flops | bytes accessed | tf_op | source)
XLA Modules:
  0.0 827.5 jit_solution(12113788238089828121)
XLA Ops:
  8.0 2.2 fusion.28
  10.2 1.9 fusion.29
  12.4 5.5 all_gather.15
  18.1 4.6 all_gather.16
  22.7 1.4 copy.34
  24.1 2.7 fusion.58
  27.5 3.4 fusion.33
  30.9 2.4 scatter.6
  33.3 155.7 %while.37 = (s32[]{:T(128)}, bf16[4096,256]{1,0:T(8,128)(2,1)}, bf16[4,128,4096]{2,1,0:T(8,128)(2,1)}, f32[4,4096]{1,0:T(4,128)S(1)}, f32[128]{0:T(128)S(1)}, /*...) while((s32[]{:T(128)}, bf16[4096,256]{1,0:T(8,128)(2,1)}, ...), condition=%wide.region_8.9_spmd, body=%wide.region_5.8_spmd.sunk | while | flops 544206912 | bytes 27970340 | solution.py:108
  33.3 2.2 collective-permute-start
  38.9 42.1 %collective-permute-done = bf16[4096,256]{1,0:T(8,128)(2,1)S(1)} collective-permute-done((bf16[4096,256]{1,0:T(8,128)(2,1)}, bf16[4096,256]{1,0:T(8,128)(2,1)S(1)}, u32[]{:S(2)}, u32[]{:S(2)}) %collective-permute-start) | collective-permute-done | bytes 2097184 | tf_op jit(solution)/shard_map/while/body/eval_jaxpr/ppermute | solution.py:15
  83.1 1.6 bitcast_dynamic-update-slice_fusion.2
  85.0 1.4 copy.44
  89.8 43.0 %collective-permute-done = bf16[4096,256]{1,0:T(8,128)(2,1)S(1)} collective-permute-done((bf16[4096,256]{1,0:T(8,128)(2,1)}, bf16[4096,256]{1,0:T(8,128)(2,1)S(1)}, u32[]{:S(2)}, u32[]{:S(2)}) %collective-permute-start) | collective-permute-done | bytes 2097184 | tf_op jit(solution)/shard_map/while/body/eval_jaxpr/ppermute | solution.py:15
  134.9 1.6 bitcast_dynamic-update-slice_fusion.2
  136.8 1.4 copy.44
  141.6 42.1 %collective-permute-done = bf16[4096,256]{1,0:T(8,128)(2,1)S(1)} collective-permute-done((bf16[4096,256]{1,0:T(8,128)(2,1)}, bf16[4096,256]{1,0:T(8,128)(2,1)S(1)}, u32[]{:S(2)}, u32[]{:S(2)}) %collective-permute-start) | collective-permute-done | bytes 2097184 | tf_op jit(solution)/shard_map/while/body/eval_jaxpr/ppermute | solution.py:15
  185.8 1.6 bitcast_dynamic-update-slice_fusion.2
  187.6 1.4 copy.44
  189.9 15.0 %all-gather = f32[8,1,16384]{2,1,0:T(1,128)S(1)} all-gather(f32[1,1,16384]{2,1,0:T(1,128)S(1)} %reshape.135), channel_id=1, replica_groups=mesh['groups'=2,'blk'=4,'dp'=2,'sub'=2] {'blk','sub'}, dimensions={0}, use_global_device_ids=true | all-gather | bytes 589824 | tf_op jit(solution)/shard_map/all_gather | solution.py:118
  206.3 3.1 fusion.16
  209.4 4.9 psum.29
  214.3 3.2 fusion.17
  218.5 15.2 %all-gather.1 = f32[8,1,16384]{2,1,0:T(1,128)S(1)} all-gather(f32[1,1,16384]{2,1,0:T(1,128)S(1)} %reshape.137), channel_id=1, replica_groups=mesh['groups'=2,'blk'=4,'dp'=2,'sub'=2] {'blk','sub'}, dimensions={0}, use_global_device_ids=true | all-gather | bytes 589824 | tf_op jit(solution)/shard_map/all_gather | solution.py:118
  235.0 3.1 fusion.18
  238.1 4.9 psum.30
  243.0 3.2 fusion.19
  247.2 15.0 %all-gather.2 = f32[8,1,16384]{2,1,0:T(1,128)S(1)} all-gather(f32[1,1,16384]{2,1,0:T(1,128)S(1)} %reshape.139), channel_id=1, replica_groups=mesh['groups'=2,'blk'=4,'dp'=2,'sub'=2] {'blk','sub'}, dimensions={0}, use_global_device_ids=true | all-gather | bytes 589824 | tf_op jit(solution)/shard_map/all_gather | solution.py:118
  263.5 3.2 fusion.20
  266.8 4.9 all-reduce.2
  271.7 2.5 fusion.27
  274.2 2.7 fusion.60
  277.4 442.2 %while.38 = (s32[]{:T(128)}, bf16[4096,256]{1,0:T(8,128)(2,1)S(1)}, f32[128,256]{1,0:T(8,128)S(1)}, f32[4096,256]{1,0:T(8,128)}, s32[3]{0:T(128)S(1)}, /*index=5...) while((s32[]{:T(128)}, bf16[4096,256]{1,0:T(8,128)(2,1)S(1)}, ...), condition=%wide.region_22.24_spmd, body=%wide.region_21.23_spmd.sunk | while | flops 811630720 | bytes 64407448 | solution.py:167
  282.0 134.1 %collective-permute-done.1 = bf16[4096,256]{1,0:T(8,128)(2,1)S(1)} collective-permute-done((bf16[4096,256]{1,0:T(8,128)(2,1)}, bf16[4096,256]{1,0:T(8,128)(2,1)S(1)}, u32[]{:S(2)}, u32[]{:S(2)}) %collective-permute-start.1) | collective-permute-done | bytes 2097184 | tf_op jit(solution)/shard_map/while/body/eval_jaxpr/ppermute | solution.py:15
  416.1 1.3 copy.57
  417.7 2.5 fusion.98
  420.7 5.1 convolution_add_fusion.7
  425.8 1.3 copy-done.2
  430.4 133.1 %collective-permute-done.1 = bf16[4096,256]{1,0:T(8,128)(2,1)S(1)} collective-permute-done((bf16[4096,256]{1,0:T(8,128)(2,1)}, bf16[4096,256]{1,0:T(8,128)(2,1)S(1)}, u32[]{:S(2)}, u32[]{:S(2)}) %collective-permute-start.1) | collective-permute-done | bytes 2097184 | tf_op jit(solution)/shard_map/while/body/eval_jaxpr/ppermute | solution.py:15
  563.5 1.3 copy.57
  565.1 2.5 fusion.98
  568.1 5.1 convolution_add_fusion.7
  577.8 132.2 %collective-permute-done.1 = bf16[4096,256]{1,0:T(8,128)(2,1)S(1)} collective-permute-done((bf16[4096,256]{1,0:T(8,128)(2,1)}, bf16[4096,256]{1,0:T(8,128)(2,1)S(1)}, u32[]{:S(2)}, u32[]{:S(2)}) %collective-permute-start.1) | collective-permute-done | bytes 2097184 | tf_op jit(solution)/shard_map/while/body/eval_jaxpr/ppermute | solution.py:15
  710.0 1.3 copy.57
  711.5 2.5 fusion.98
  714.6 5.1 convolution_add_fusion.7
  720.4 90.3 %collective-permute-done.3 = f32[4096,256]{1,0:T(8,128)} collective-permute-done((f32[4096,256]{1,0:T(8,128)}, f32[4096,256]{1,0:T(8,128)}, u32[]{:S(2)}, u32[]{:S(2)}) %collective-permute-start.3) | collective-permute-done | bytes 4194336 | tf_op jit(solution)/shard_map/ppermute | solution.py:15
  810.7 10.0 %reduce-scatter.5.cloned.1.call-done = f32[2048,256]{1,0:T(8,128)} async-done(((f32[4096,256]{1,0:T(8,128)}), f32[2048,256]{1,0:T(8,128)}) %reduce-scatter.5.cloned.1.call-update) | async-done | bytes 2097168 | tf_op jit(solution)/shard_map/reduce_scatter | solution.py:170
  (121 shorter events, 25.8 us)
Async XLA Ops:
  7.2 803.5 %reduce-scatter.3.cloned.1.call-start = ((), (), s32[]{:S(2)}) async-start(), calls=%async_computation.2 | async-start | bytes 196608 | tf_op jit(solution)/shard_map/reduce_scatter | solution.py:169
  10.2 2.0 copy-start.5
  10.2 7.7 copy-start.6
  12.2 11.9 %copy-start = (bf16[4096,256]{1,0:T(8,128)(2,1)}, bf16[4096,256]{1,0:T(8,128)(2,1)S(1)}, u32[]{:S(2)}) copy-start(bf16[4096,256]{1,0:T(8,128)(2,1)S(1)} %fusion.29) | copy-start | bytes 6291460
  24.1 2.9 copy-start.7
  33.3 47.7 %collective-permute-start = (bf16[4096,256]{1,0:T(8,128)(2,1)}, bf16[4096,256]{1,0:T(8,128)(2,1)S(1)}, u32[]{:S(2)}, u32[]{:S(2)}) collective-permute-start(bf16[4096,256]{1,0:T(8,128)(2,1)} %get-tuple-element.575), channel_id=1, source_target_pairs={{12,0},{0,4},{4,8},{8,12},{13,1},{1,5},{5,9},{9,13},{14,2},{2,6},{... | collective-permute-start | bytes 6291464 | tf_op jit(solution)/shard_map/while/body/eval_jaxpr/ppermute | solution.py:15
  86.4 46.4 %collective-permute-start = (bf16[4096,256]{1,0:T(8,128)(2,1)}, bf16[4096,256]{1,0:T(8,128)(2,1)S(1)}, u32[]{:S(2)}, u32[]{:S(2)}) collective-permute-start(bf16[4096,256]{1,0:T(8,128)(2,1)} %get-tuple-element.575), channel_id=1, source_target_pairs={{12,0},{0,4},{4,8},{8,12},{13,1},{1,5},{5,9},{9,13},{14,2},{2,6},{... | collective-permute-start | bytes 6291464 | tf_op jit(solution)/shard_map/while/body/eval_jaxpr/ppermute | solution.py:15
  138.2 45.5 %collective-permute-start = (bf16[4096,256]{1,0:T(8,128)(2,1)}, bf16[4096,256]{1,0:T(8,128)(2,1)S(1)}, u32[]{:S(2)}, u32[]{:S(2)}) collective-permute-start(bf16[4096,256]{1,0:T(8,128)(2,1)} %get-tuple-element.575), channel_id=1, source_target_pairs={{12,0},{0,4},{4,8},{8,12},{13,1},{1,5},{5,9},{9,13},{14,2},{2,6},{... | collective-permute-start | bytes 6291464 | tf_op jit(solution)/shard_map/while/body/eval_jaxpr/ppermute | solution.py:15
  263.5 8.2 copy-start.1
  277.5 1.3 copy-start.2
  277.5 143.2 %collective-permute-start.2 = (f32[4096,256]{1,0:T(8,128)}, f32[4096,256]{1,0:T(8,128)}, u32[]{:S(2)}, u32[]{:S(2)}) collective-permute-start(f32[4096,256]{1,0:T(8,128)} %get-tuple-element.628), channel_id=1, source_target_pairs={{12,0},{0,4},{4,8},{8,12},{13,1},{1,5},{5,9},{9,13},{14,2},{2,6},{... | collective-permute-start | bytes 12582920 | tf_op jit(solution)/shard_map/while/body/eval_jaxpr/ppermute | solution.py:15
  278.8 137.4 %collective-permute-start.1 = (bf16[4096,256]{1,0:T(8,128)(2,1)}, bf16[4096,256]{1,0:T(8,128)(2,1)S(1)}, u32[]{:S(2)}, u32[]{:S(2)}) collective-permute-start(bf16[4096,256]{1,0:T(8,128)(2,1)} %copy-done.2), channel_id=1, source_target_pairs={{12,0},{0,4},{4,8},{8,12},{13,1},{1,5},{5,9},{9,13},{14,2},{2,6},{... | collective-permute-start | bytes 6291464 | tf_op jit(solution)/shard_map/while/body/eval_jaxpr/ppermute | solution.py:15
  420.7 5.1 copy-start.3
  425.8 1.3 copy-start.2
  425.8 142.3 %collective-permute-start.2 = (f32[4096,256]{1,0:T(8,128)}, f32[4096,256]{1,0:T(8,128)}, u32[]{:S(2)}, u32[]{:S(2)}) collective-permute-start(f32[4096,256]{1,0:T(8,128)} %get-tuple-element.628), channel_id=1, source_target_pairs={{12,0},{0,4},{4,8},{8,12},{13,1},{1,5},{5,9},{9,13},{14,2},{2,6},{... | collective-permute-start | bytes 12582920 | tf_op jit(solution)/shard_map/while/body/eval_jaxpr/ppermute | solution.py:15
  427.1 136.4 %collective-permute-start.1 = (bf16[4096,256]{1,0:T(8,128)(2,1)}, bf16[4096,256]{1,0:T(8,128)(2,1)S(1)}, u32[]{:S(2)}, u32[]{:S(2)}) collective-permute-start(bf16[4096,256]{1,0:T(8,128)(2,1)} %copy-done.2), channel_id=1, source_target_pairs={{12,0},{0,4},{4,8},{8,12},{13,1},{1,5},{5,9},{9,13},{14,2},{2,6},{... | collective-permute-start | bytes 6291464 | tf_op jit(solution)/shard_map/while/body/eval_jaxpr/ppermute | solution.py:15
  568.1 5.1 copy-start.3
  573.2 1.3 copy-start.2
  573.2 141.4 %collective-permute-start.2 = (f32[4096,256]{1,0:T(8,128)}, f32[4096,256]{1,0:T(8,128)}, u32[]{:S(2)}, u32[]{:S(2)}) collective-permute-start(f32[4096,256]{1,0:T(8,128)} %get-tuple-element.628), channel_id=1, source_target_pairs={{12,0},{0,4},{4,8},{8,12},{13,1},{1,5},{5,9},{9,13},{14,2},{2,6},{... | collective-permute-start | bytes 12582920 | tf_op jit(solution)/shard_map/while/body/eval_jaxpr/ppermute | solution.py:15
  574.5 135.5 %collective-permute-start.1 = (bf16[4096,256]{1,0:T(8,128)(2,1)}, bf16[4096,256]{1,0:T(8,128)(2,1)S(1)}, u32[]{:S(2)}, u32[]{:S(2)}) collective-permute-start(bf16[4096,256]{1,0:T(8,128)(2,1)} %copy-done.2), channel_id=1, source_target_pairs={{12,0},{0,4},{4,8},{8,12},{13,1},{1,5},{5,9},{9,13},{14,2},{2,6},{... | collective-permute-start | bytes 6291464 | tf_op jit(solution)/shard_map/while/body/eval_jaxpr/ppermute | solution.py:15
  714.5 5.1 copy-start.3
  719.6 0.6 copy-start.4
  719.6 91.0 %collective-permute-start.3 = (f32[4096,256]{1,0:T(8,128)}, f32[4096,256]{1,0:T(8,128)}, u32[]{:S(2)}, u32[]{:S(2)}) collective-permute-start(f32[4096,256]{1,0:T(8,128)} %get-tuple-element.360), channel_id=1, source_target_pairs={{12,0},{0,4},{4,8},{8,12},{13,1},{1,5},{5,9},{9,13},{14,2},{2,6},{... | collective-permute-start | bytes 12582920 | tf_op jit(solution)/shard_map/ppermute | solution.py:15
  720.3 100.4 %reduce-scatter.5.cloned.1.call-start = ((), (), s32[]{:S(2)}) async-start(), calls=%async_computation.3 | async-start | bytes 6291456 | tf_op jit(solution)/shard_map/reduce_scatter | solution.py:170
Sparse Core Ops, SparseCore 0:
  720.4 10.6 reduce-scatter.2
  810.8 9.8 reduce-scatter.4
